TPU v7x, 512 devices: a whole 4x8x8 slice. The times are simulated.
512 devices in a mesh: seq: 64 (over x, z, core), rep: 8 (over y).
Axes of the slice: x: 4, y: 8, z: 8, core: 2. Of those that a mesh axis runs over, the one named last changes fastest.
Arguments:
- token_ids: int32 [32, 4], P('rep'), parts along dimension 0, may hold values from 0 to 24703
- cache_lengths: int32 [32], P('rep'), parts along dimension 0, may hold values from 1 to 8192, 8216 in all
- embed_table: bfloat16 [2048, 24704], P('seq'), may hold values from -0.119628906 to 0.119628906
- key_cache: bfloat16 [32, 8192, 512], P('rep', 'seq'), parts along dimension 0, may hold values from -4000 to 4000
- value_cache: bfloat16 [32, 8192, 512], P('rep', 'seq'), parts along dimension 0, may hold values from -24 to 24
- norm_attn: bfloat16 [2048], replicated, may hold values from 0.25 to 1.75
- norm_mlp: bfloat16 [2048], replicated, may hold values from 0.25 to 1.75
- w_qkv: bfloat16 [2048, 3072], P(None, 'seq'), may hold values from -0.125 to 0.125
- w_out: bfloat16 [2048, 2048], P(None, 'seq'), may hold values from -0.125 to 0.125
- w_gate: bfloat16 [2048, 8192], P(None, 'seq'), may hold values from -0.125 to 0.125
- w_up: bfloat16 [2048, 8192], P(None, 'seq'), may hold values from -0.125 to 0.125
- w_down: bfloat16 [8192, 2048], P('seq'), may hold values from -0.0625 to 0.0625
Outputs:
- layer_out: bfloat16 [32, 4, 2048], P('rep'), parts along dimension 0
There are 8 independent parts, one for each index of `rep`. A program takes and returns all parts, laid end to end along the dimension named above; an argument that names none is the same for every part. Nothing has to cross between parts.
All inputs are finite; a program needn't handle non-finite values.
Results may differ from a plain program's by a relative error of at most 0.012.
The roundings to bfloat16 on the way count: a program that leaves them out, or rounds other values in their place, can miss the bound.
Values may be sent and summed in bfloat16 or wider, within the bound.
A program may use at most 128 MiB of HBM per device.

v0:
```python
import jax
import jax.numpy as jnp
from jax import lax
from jax.sharding import PartitionSpec as P

H = 32
KVH = 8
HD = 64
STEPS = 4
norm_epsilon = 1e-05
embed_factor = 12.0
score_factor = 0.015625
branch_factor = 0.22
rope_base = 10000000.0
masked_floor = -1e30


def rms_scale(resid, gain):
    mean_square = jnp.mean(resid * resid, axis=-1, keepdims=True)
    return resid * lax.rsqrt(mean_square + norm_epsilon) * gain.astype(jnp.float32)


def rotate(vectors, where):
    half = vectors.shape[-1] // 2
    freqs = rope_base ** (-2.0 * jnp.arange(half, dtype=jnp.float32) / vectors.shape[-1])
    angle = where[..., None] * freqs
    cosine = jnp.cos(angle)
    sine = jnp.sin(angle)
    first_half = vectors[..., :half]
    second_half = vectors[..., half:]
    return jnp.concatenate(
        [first_half * cosine - second_half * sine, second_half * cosine + first_half * sine],
        axis=-1,
    )


def partial_softmax(queries, keys, values, valid):
    scores = (
        jnp.einsum("rskgd,rpkd->rskgp", queries, keys, preferred_element_type=jnp.float32)
        * score_factor
    )
    maxima = jnp.max(jnp.where(valid, scores, masked_floor), axis=-1)
    expo = jnp.exp(jnp.where(valid, scores - maxima[..., None], masked_floor))
    totals = jnp.sum(expo, axis=-1)
    outputs = jnp.einsum(
        "rskgp,rpkd->rskgd", expo.astype(jnp.bfloat16), values, preferred_element_type=jnp.float32
    )
    return (maxima, totals, outputs)


def shards(
    token_ids,
    cache_lengths,
    embed_table,
    key_cache,
    value_cache,
    norm_attn,
    norm_mlp,
    w_qkv,
    w_out,
    w_gate,
    w_up,
    w_down,
):
    place = lax.axis_index("seq")
    req_all = token_ids.shape[0]
    steps = token_ids.shape[1]
    ctx_own = key_cache.shape[1]
    att_width = H * HD
    kv_width = KVH * HD
    group = H // KVH
    picked = jnp.take(embed_table, token_ids.reshape(-1), axis=1)
    whole = lax.all_gather(picked, "seq", axis=0, tiled=True)
    resid = (
        jnp.transpose(whole, (1, 0)).reshape(req_all, steps, -1).astype(jnp.float32) * embed_factor
    )
    slot_pos = place * ctx_own + jnp.arange(ctx_own, dtype=jnp.int32)
    cache_valid = (slot_pos[None, :] < cache_lengths[:, None]).reshape(req_all, 1, 1, 1, ctx_own)
    cache_keys = key_cache.reshape(req_all, ctx_own, KVH, HD)
    cache_values = value_cache.reshape(req_all, ctx_own, KVH, HD)
    normed = rms_scale(resid, norm_attn).astype(jnp.bfloat16)
    qkv_cols = jnp.einsum("rsd,dc->rsc", normed, w_qkv, preferred_element_type=jnp.float32).astype(
        jnp.bfloat16
    )
    qkv_all = lax.all_gather(qkv_cols, "seq", axis=2, tiled=True)
    where = (cache_lengths[:, None] + jnp.arange(steps, dtype=jnp.int32)[None, :]).astype(
        jnp.float32
    )
    queries = rotate(
        qkv_all[..., :att_width].reshape(req_all, steps, H, HD).astype(jnp.float32),
        where[..., None],
    ).astype(jnp.bfloat16)
    keys_new = rotate(
        qkv_all[..., att_width : att_width + kv_width]
        .reshape(req_all, steps, KVH, HD)
        .astype(jnp.float32),
        where[..., None],
    ).astype(jnp.bfloat16)
    values_new = qkv_all[..., att_width + kv_width :].reshape(req_all, steps, KVH, HD)
    grouped = queries.reshape(req_all, steps, KVH, group, HD)
    cache_max, cache_total, cache_out = partial_softmax(
        grouped, cache_keys, cache_values, cache_valid
    )
    fresh_valid = (
        jnp.arange(steps, dtype=jnp.int32)[None, :] <= jnp.arange(steps, dtype=jnp.int32)[:, None]
    ).reshape(1, steps, 1, 1, steps)
    fresh_max, fresh_total, fresh_out = partial_softmax(grouped, keys_new, values_new, fresh_valid)
    overall = jnp.maximum(lax.pmax(cache_max, "seq"), fresh_max)
    cache_scale = jnp.exp(cache_max - overall)
    packed = jnp.concatenate(
        [cache_scale[..., None] * cache_out, (cache_scale * cache_total)[..., None]], axis=-1
    )
    summed = lax.psum(packed, "seq")
    fresh_scale = jnp.exp(fresh_max - overall)
    numer = summed[..., :HD] + fresh_scale[..., None] * fresh_out
    denom = summed[..., HD] + fresh_scale * fresh_total
    attention = (numer / denom[..., None]).astype(jnp.bfloat16).reshape(req_all, steps, att_width)
    proj_cols = jnp.einsum(
        "rsa,ac->rsc", attention, w_out, preferred_element_type=jnp.float32
    ).astype(jnp.bfloat16)
    projected = lax.all_gather(proj_cols, "seq", axis=2, tiled=True)
    middle = resid + branch_factor * projected.astype(jnp.float32)
    normed_mlp = rms_scale(middle, norm_mlp).astype(jnp.bfloat16)
    gate = jnp.einsum("rsd,df->rsf", normed_mlp, w_gate, preferred_element_type=jnp.float32)
    upward = jnp.einsum("rsd,df->rsf", normed_mlp, w_up, preferred_element_type=jnp.float32)
    hidden = (jax.nn.silu(gate) * upward).astype(jnp.bfloat16)
    down_part = jnp.einsum("rsf,fd->rsd", hidden, w_down, preferred_element_type=jnp.float32)
    down = lax.psum(down_part, "seq")
    return (middle + branch_factor * down).astype(jnp.bfloat16)


def solution(mesh):
    return jax.shard_map(
        shards,
        mesh=mesh,
        in_specs=(
            P("rep", None),
            P("rep"),
            P("seq", None),
            P("rep", "seq", None),
            P("rep", "seq", None),
            P(),
            P(),
            P(None, "seq"),
            P(None, "seq"),
            P(None, "seq"),
            P(None, "seq"),
            P("seq", None),
        ),
        out_specs=P("rep", None, None),
        check_vma=False,
    )
```

profile of v0, /device:TPU:1, one launch (start us, length us, event | category | flops | bytes accessed | tf_op | source)
XLA Modules:
  0.0 811.6 jit_solution(16249509916441426397)
XLA Ops:
  6.5 0.0 copy-start
  6.5 0.0 all-reduce.3.cloned.1.call-start
  6.5 0.8 reshape.176
  7.4 0.8 reshape.175
  8.1 0.0 copy-start.7
  8.2 6.4 copy.89
  14.6 4.2 gather_fusion
  18.8 0.1 select_bitcast_fusion
  18.9 51.6 %all-gather = bf16[64,32,16]{1,2,0:T(8,128)(2,1)S(1)} all-gather(bf16[1,32,16]{1,2,0:T(8,128)(2,1)S(1)} %select_bitcast_fusion), channel_id=1, replica_groups=mesh['seq'=64,'rep'=8] {'seq'}, dimensions={0}, use_global_device_ids=true | all-gather | bytes 66560 | tf_op jit(solution)/shard_map/all_gather | solution.py:73
  70.4 0.3 copy.90
  70.8 0.2 copy.91
  71.0 0.2 reshape.194
  71.2 0.1 multiply_reduce_fusion.1
  71.4 0.1 mul.209
  71.5 0.0 copy-done.4
  71.5 0.0 copy-done.7
  71.5 0.2 convolution_convert_fusion.1
  71.7 0.1 copy.92
  71.9 51.1 %all_gather.10 = bf16[4,4,3072]{1,0,2:T(4,128)(2,1)S(1)} all-gather(bf16[4,4,48]{1,0,2:T(4,128)(2,1)S(1)} %copy.92), channel_id=1, replica_groups=mesh['seq'=64,'rep'=8] {'seq'}, dimensions={2}, use_global_device_ids=true | all-gather | bytes 99840 | tf_op jit(solution)/shard_map/all_gather | solution.py:85
  123.0 0.7 slice.38
  123.8 0.0 copy-start.6
  123.8 1.2 fusion.44
  124.9 2.2 copy.124
  127.1 1.0 reshape.182
  128.1 0.0 copy-done.6
  128.2 0.1 add_convert_fusion.3
  128.2 0.3 copy.125
  128.5 0.1 reshape.183
  128.6 0.1 fusion.45
  128.7 0.1 broadcast_compare_fusion
  128.8 1.3 copy.96
  130.1 0.1 multiply_cosine_fusion
  130.3 0.1 subtract_convert_fusion
  130.4 0.2 pad_maximum_fusion.1
  130.6 0.4 select_reduce_fusion.1
  131.0 243.2 %pmax.7 = f32[4,4,8,4]{3,1,2,0:T(4,128)S(1)} all-reduce(f32[4,4,8,4]{3,1,2,0:T(4,128)S(1)} %get-tuple-element.19), channel_id=1, replica_groups=mesh['seq'=64,'rep'=8] {'seq'}, use_global_device_ids=true, to_apply=%region_2.3 | all-reduce | flops 512 | bytes 4096 | tf_op jit(solution)/shard_map/pmax | solution.py:108
  374.2 0.4 fusion.16
  374.7 0.3 copy.100
  375.0 1.3 select_reduce_fusion
  376.3 0.0 copy-start.5
  376.4 0.9 copy.102
  377.3 0.5 fusion.1
  377.7 0.9 pad_maximum_fusion
  378.7 0.0 all-reduce.3.cloned.1.call-update
  378.7 0.2 all-reduce.5.cloned.1.call-start
  378.9 0.4 fusion.18
  379.3 0.0 copy-done.5
  379.3 0.0 copy-start.8
  379.3 185.2 %all-reduce.3.cloned.1.call-done = f32[4,4,8,4,65]{4,3,1,2,0:T(4,128)} async-done(((f32[4,4,8,4,65]{4,3,1,2,0:T(4,128)}), f32[4,4,8,4,65]{4,3,1,2,0:T(4,128)}) %all-reduce.3.cloned.1.call-update) | async-done | bytes 133136 | tf_op jit(solution)/shard_map/psum | solution.py:113
  564.5 1.1 slice.46
  565.7 0.9 copy.123
  566.6 1.6 fusion.6
  568.2 0.0 copy-start.2
  568.3 0.1 reshape.180
  568.4 0.2 convolution_convert_fusion
  568.6 0.1 copy.109
  568.7 48.3 %all_gather.11 = bf16[4,4,2048]{1,0,2:T(4,128)(2,1)S(1)} all-gather(bf16[4,4,32]{1,0,2:T(4,128)(2,1)S(1)} %copy.109), channel_id=1, replica_groups=mesh['seq'=64,'rep'=8] {'seq'}, dimensions={2}, use_global_device_ids=true | all-gather | bytes 66560 | tf_op jit(solution)/shard_map/all_gather | solution.py:121
  617.0 1.3 copy.110
  618.3 0.1 multiply_reduce_fusion
  618.5 1.3 fusion.12
  619.8 1.1 fusion.8
  620.9 0.0 all-reduce.5.cloned.1.call-update
  620.9 182.2 %all-reduce.5.cloned.1.call-done = f32[4,4,2048]{2,1,0:T(4,128)} async-done(((f32[4,4,2048]{2,1,0:T(4,128)}), f32[4,4,2048]{2,1,0:T(4,128)}) %all-reduce.5.cloned.1.call-update) | async-done | bytes 131088 | tf_op jit(solution)/shard_map/psum | solution.py:128
  803.2 1.6 add_convert_fusion.1
  (23 shorter events, 0.3 us)
Async XLA Ops:
  6.5 613.2 %copy-start = (bf16[128,2048]{1,0:T(8,128)(2,1)S(1)}, bf16[128,2048]{1,0:T(8,128)(2,1)}, u32[]{:S(2)}) copy-start(bf16[128,2048]{1,0:T(8,128)(2,1)} %param.23) | copy-start | bytes 1572868
  6.5 558.0 %all-reduce.3.cloned.1.call-start = ((), (), s32[]{:S(2)}) async-start(), calls=%async_computation | async-start | bytes 524288 | tf_op jit(solution)/shard_map/psum | solution.py:113
  8.1 63.3 %copy-start.4 = (bf16[2048]{0:T(1024)(128)(2,1)S(1)}, bf16[2048]{0:T(1024)(128)(2,1)}, u32[]{:S(2)}) copy-start(bf16[2048]{0:T(1024)(128)(2,1)} %param.17) | copy-start | bytes 12292
  8.1 63.3 %copy-start.7 = (bf16[2048,48]{0,1:T(8,128)(2,1)S(1)}, bf16[2048,48]{0,1:T(8,128)(2,1)}, u32[]{:S(2)}) copy-start(bf16[2048,48]{0,1:T(8,128)(2,1)} %param.19) | copy-start | bytes 589828
  123.8 4.4 copy-start.6
  127.1 247.6 %copy-start.1 = (bf16[4,128,512]{2,1,0:T(8,128)(2,1)S(1)}, bf16[4,128,512]{2,1,0:T(8,128)(2,1)}, u32[]{:S(2)}) copy-start(bf16[4,128,512]{2,1,0:T(8,128)(2,1)} %param.16) | copy-start | bytes 1572868
  376.3 3.0 copy-start.5
  377.3 189.3 %copy-start.3 = (bf16[4,4,512]{1,0,2:T(4,128)(2,1)S(1)}, bf16[4,4,512]{1,0,2:T(4,128)(2,1)}, u32[]{:S(2)}) copy-start(bf16[4,4,512]{1,0,2:T(4,128)(2,1)} %get-tuple-element.10) | copy-start | bytes 49156
  378.7 424.5 %all-reduce.5.cloned.1.call-start = ((), (), s32[]{:S(2)}) async-start(), calls=%async_computation.1 | async-start | bytes 262144 | tf_op jit(solution)/shard_map/psum | solution.py:128
  379.3 189.1 %copy-start.8 = (bf16[2048,32]{0,1:T(8,128)(2,1)S(1)}, bf16[2048,32]{0,1:T(8,128)(2,1)}, u32[]{:S(2)}) copy-start(bf16[2048,32]{0,1:T(8,128)(2,1)} %param.20) | copy-start | bytes 393220
  568.2 51.6 %copy-start.2 = (bf16[2048,128]{1,0:T(8,128)(2,1)S(1)}, bf16[2048,128]{1,0:T(8,128)(2,1)}, u32[]{:S(2)}) copy-start(bf16[2048,128]{1,0:T(8,128)(2,1)} %param.22) | copy-start | bytes 1572868
Sparse Core Ops, SparseCore 0:
  378.8 185.6 all-reduce.2
  621.0 182.0 all-reduce.4
where the time goes:
time: 812 us
  blocking collectives  394 us (49%)
  waiting for transfers between devices  368 us (45%)
  local copies, waits for them, and re-layouts  24.9 us (3%)
  between operations  13.7 us (2%)
    pmax x1, blocking collectives, shards(): overall = jnp.maximum(lax.pmax(cache_max, 'seq'), fresh_max)  243 us
    psum x1, waiting for transfers between devices, shards(): summed = lax.psum(packed, 'seq')  185 us
    psum x1, waiting for transfers between devices, shards(): down = lax.psum(down_part, 'seq')  182 us
    all_gather x1, blocking collectives, shards(): whole = lax.all_gather(picked, 'seq', axis=0, tiled=True)  51.6 us
    all_gather x1, blocking collectives, shards(): qkv_all = lax.all_gather(qkv_cols, 'seq', axis=2, tiled=True)  51.1 us
    all_gather x1, blocking collectives, shards(): projected = lax.all_gather(proj_cols, 'seq', axis=2, tiled=True)  48.3 us
  transfers between devices with their start and end apart: 2, of which 2 were waited for; matrix products, arithmetic and copies ran while one was open for 0% of the time, Pallas kernels for 0%

commit v1 on v0

--- a/solution.py
+++ b/solution.py
@@ -125,7 +125,7 @@
     upward = jnp.einsum("rsd,df->rsf", normed_mlp, w_up, preferred_element_type=jnp.float32)
     hidden = (jax.nn.silu(gate) * upward).astype(jnp.bfloat16)
     down_part = jnp.einsum("rsf,fd->rsd", hidden, w_down, preferred_element_type=jnp.float32)
-    down = lax.psum(down_part, "seq")
+    down = jnp.sum(lax.all_gather(down_part, "seq"), axis=0)
     return (middle + branch_factor * down).astype(jnp.bfloat16)
 
 

time: 812 us -> 724 us (0.89)
  waiting for transfers between devices: 368 us -> 273 us
    psum x1 -> x0, waiting for transfers between devices: 182 us -> none  [shards(): down = lax.psum(down_part, 'seq')]
    all_gather x0 -> x1, waiting for transfers between devices: none -> 87.5 us  [shards(): down = jnp.sum(lax.all_gather(down_part, 'seq'), axis=0)]
where the time goes in v1:
time: 724 us
  blocking collectives  394 us (54%)
  waiting for transfers between devices  273 us (38%)
  local copies, waits for them, and re-layouts  25.7 us (4%)
  between operations  13.7 us (2%)
  other arithmetic  9.65 us (1%)
  matrix products  7.54 us (1%)
    pmax x1, blocking collectives, shards(): overall = jnp.maximum(lax.pmax(cache_max, 'seq'), fresh_max)  243 us
    psum x1, waiting for transfers between devices, shards(): summed = lax.psum(packed, 'seq')  185 us
    all_gather x1, waiting for transfers between devices, shards(): down = jnp.sum(lax.all_gather(down_part, 'seq'), axis=0)  87.5 us
    all_gather x1, blocking collectives, shards(): whole = lax.all_gather(picked, 'seq', axis=0, tiled=True)  51.6 us
    all_gather x1, blocking collectives, shards(): qkv_all = lax.all_gather(qkv_cols, 'seq', axis=2, tiled=True)  51.1 us
    all_gather x1, blocking collectives, shards(): projected = lax.all_gather(proj_cols, 'seq', axis=2, tiled=True)  48.3 us
  transfers between devices with their start and end apart: 2, of which 2 were waited for; matrix products, arithmetic and copies ran while one was open for 0% of the time, Pallas kernels for 0%

profile of v1, /device:TPU:1, one launch (start us, length us, event | category | flops | bytes accessed | tf_op | source)
XLA Modules:
  0.0 723.8 jit_solution(8158428959284720622)
XLA Ops:
  6.5 0.0 copy-start
  6.5 0.0 all-reduce.2.cloned.1.call-start
  6.5 0.8 reshape.176
  7.4 0.8 reshape.175
  8.2 0.7 convert_element_type.75
  8.9 6.4 copy.116
  15.3 4.2 gather_fusion
  19.5 0.1 select_bitcast_fusion
  19.5 51.6 %all-gather.1 = bf16[64,32,16]{1,2,0:T(8,128)(2,1)S(1)} all-gather(bf16[1,32,16]{1,2,0:T(8,128)(2,1)S(1)} %select_bitcast_fusion), channel_id=1, replica_groups=mesh['seq'=64,'rep'=8] {'seq'}, dimensions={0}, use_global_device_ids=true | all-gather | bytes 66560 | tf_op jit(solution)/shard_map/all_gather | solution.py:73
  71.1 0.3 copy.117
  71.4 0.2 copy.118
  71.6 0.2 reshape.195
  71.9 0.1 multiply_reduce_fusion.1
  72.0 0.1 mul.209
  72.2 0.0 copy-done.6
  72.2 0.2 convolution_convert_fusion.1
  72.4 0.1 copy.119
  72.6 51.1 %all_gather.16 = bf16[4,4,3072]{1,0,2:T(4,128)(2,1)S(1)} all-gather(bf16[4,4,48]{1,0,2:T(4,128)(2,1)S(1)} %copy.119), channel_id=1, replica_groups=mesh['seq'=64,'rep'=8] {'seq'}, dimensions={2}, use_global_device_ids=true | all-gather | bytes 99840 | tf_op jit(solution)/shard_map/all_gather | solution.py:85
  123.7 1.2 fusion.44
  124.8 0.7 slice.38
  125.6 0.0 copy-done.5
  125.6 0.1 add_convert_fusion.3
  125.7 0.1 broadcast_compare_fusion
  125.8 2.1 copy.123
  127.8 2.1 copy.127
  129.9 1.3 copy.151
  131.2 0.3 copy.152
  131.5 0.1 reshape.183
  131.6 0.1 fusion.45
  131.7 0.2 reshape.182
  131.8 0.1 multiply_cosine_fusion
  132.0 0.1 subtract_convert_fusion
  132.1 0.2 pad_maximum_fusion.1
  132.3 1.4 select_reduce_fusion.1
  133.7 243.2 %pmax.7 = f32[4,4,8,4]{3,1,2,0:T(4,128)S(1)} all-reduce(f32[4,4,8,4]{3,1,2,0:T(4,128)S(1)} %get-tuple-element.19), channel_id=1, replica_groups=mesh['seq'=64,'rep'=8] {'seq'}, use_global_device_ids=true, to_apply=%region_2.3 | all-reduce | flops 512 | bytes 4096 | tf_op jit(solution)/shard_map/pmax | solution.py:108
  377.0 0.4 fusion.16
  377.5 1.3 select_reduce_fusion
  378.8 0.0 copy-start.4
  378.8 0.9 copy.129
  379.7 0.5 fusion.1
  380.2 0.9 pad_maximum_fusion
  381.1 0.0 all-reduce.2.cloned.1.call-update
  381.1 0.2 all-gather.4.cloned.1.call-start
  381.4 0.4 fusion.18
  381.7 0.0 copy-start.7
  381.8 185.2 %all-reduce.2.cloned.1.call-done = f32[4,4,8,4,65]{4,3,1,2,0:T(4,128)} async-done(((f32[4,4,8,4,65]{4,3,1,2,0:T(4,128)}), f32[4,4,8,4,65]{4,3,1,2,0:T(4,128)}) %all-reduce.2.cloned.1.call-update) | async-done | bytes 133136 | tf_op jit(solution)/shard_map/psum | solution.py:113
  567.0 1.1 slice.46
  568.1 0.9 copy.150
  569.1 1.6 fusion.6
  570.7 0.0 copy-start.1
  570.7 0.1 reshape.180
  570.9 0.2 convolution_convert_fusion
  571.0 0.1 copy.136
  571.2 48.3 %all_gather.17 = bf16[4,4,2048]{1,0,2:T(4,128)(2,1)S(1)} all-gather(bf16[4,4,32]{1,0,2:T(4,128)(2,1)S(1)} %copy.136), channel_id=1, replica_groups=mesh['seq'=64,'rep'=8] {'seq'}, dimensions={2}, use_global_device_ids=true | all-gather | bytes 66560 | tf_op jit(solution)/shard_map/all_gather | solution.py:121
  619.5 1.3 copy.137
  620.8 0.1 multiply_reduce_fusion
  620.9 1.3 fusion.12
  622.2 0.0 copy-done
  622.2 0.0 copy-done.1
  622.2 1.1 fusion.8
  623.3 0.0 all-gather.4.cloned.1.call-update
  623.4 87.5 %all-gather.4.cloned.1.call-done = f32[256,4,2048]{2,1,0:T(4,128)} async-done(((f32[4,4,2048]{2,1,0:T(4,128)}), f32[256,4,2048]{2,1,0:T(4,128)}) %all-gather.4.cloned.1.call-update) | async-done | bytes 8388624 | tf_op jit(solution)/shard_map/all_gather | solution.py:128
  710.9 5.3 reduce_sum.49
  716.2 0.7 add_convert_fusion.1
  (22 shorter events, 0.3 us)
Async XLA Ops:
  6.5 615.7 %copy-start = (bf16[128,2048]{1,0:T(8,128)(2,1)S(1)}, bf16[128,2048]{1,0:T(8,128)(2,1)}, u32[]{:S(2)}) copy-start(bf16[128,2048]{1,0:T(8,128)(2,1)} %param.23) | copy-start | bytes 1572868
  6.5 560.4 %all-reduce.2.cloned.1.call-start = ((), (), s32[]{:S(2)}) async-start(), calls=%async_computation | async-start | bytes 524288 | tf_op jit(solution)/shard_map/psum | solution.py:113
  8.9 63.3 %copy-start.6 = (bf16[2048,48]{0,1:T(8,128)(2,1)S(1)}, bf16[2048,48]{0,1:T(8,128)(2,1)}, u32[]{:S(2)}) copy-start(bf16[2048,48]{0,1:T(8,128)(2,1)} %param.19) | copy-start | bytes 589828
  123.7 1.9 copy-start.5
  131.2 248.6 %copy-start.2 = (bf16[4,128,512]{1,2,0:T(8,128)(2,1)S(1)}, bf16[4,128,512]{1,2,0:T(8,128)(2,1)}, u32[]{:S(2)}) copy-start(bf16[4,128,512]{1,2,0:T(8,128)(2,1)} %copy.127) | copy-start | bytes 1572868
  378.8 3.0 copy-start.4
  379.7 189.3 %copy-start.3 = (bf16[4,4,512]{1,0,2:T(4,128)(2,1)S(1)}, bf16[4,4,512]{1,0,2:T(4,128)(2,1)}, u32[]{:S(2)}) copy-start(bf16[4,4,512]{1,0,2:T(4,128)(2,1)} %get-tuple-element.10) | copy-start | bytes 49156
  381.1 329.7 %all-gather.4.cloned.1.call-start = ((), (), s32[]{:S(2)}) async-start(), calls=%async_computation.1 | async-start | bytes 8519680 | tf_op jit(solution)/shard_map/all_gather | solution.py:128
  381.7 189.1 %copy-start.7 = (bf16[2048,32]{0,1:T(8,128)(2,1)S(1)}, bf16[2048,32]{0,1:T(8,128)(2,1)}, u32[]{:S(2)}) copy-start(bf16[2048,32]{0,1:T(8,128)(2,1)} %param.20) | copy-start | bytes 393220
  570.7 51.6 %copy-start.1 = (bf16[2048,128]{1,0:T(8,128)(2,1)S(1)}, bf16[2048,128]{1,0:T(8,128)(2,1)}, u32[]{:S(2)}) copy-start(bf16[2048,128]{1,0:T(8,128)(2,1)} %param.22) | copy-start | bytes 1572868
Sparse Core Ops, SparseCore 0:
  381.3 185.6 all-reduce.1
  623.5 87.3 all-gather.3
